TPU v7x, 512 devices: a whole 4x8x8 slice. The times are simulated.
512 devices in a mesh: dp: 64 (over z, y_hi, core), own: 8 (over y_lo, x).
Axes of the slice: x: 4, y: 8 (y_hi: 4, y_lo: 2; y = y_hi * 2 + y_lo), z: 8, core: 2. Of those that a mesh axis runs over, the one named last changes fastest.
Arguments:
- wide_rows: bfloat16 [8, 393216, 256], P(None, ('dp', 'own'))
- narrow_rows: bfloat16 [8, 393216, 128], P(None, ('dp', 'own'))
- owner_map: int32 [8], replicated, may hold values from 0 to 7, as said below
Outputs:
- kept_inverse: float32 [16, 256, 256], P('own', None, 'dp')
- update: float32 [8, 128, 256], P(None, 'own', 'dp')
Inputs may be any that keep to these rules, and one draw needn't show every extreme that they name: owner_map[l] names the owner of layer l; no owner has more than 2 layers, and one owner has exactly 2.
All inputs are finite; a program needn't handle non-finite values.
Results may differ from a plain program's by a relative error of at most 0.0003.
Values sent between devices are 32-bit elements; how exact they have to be, the bound alone decides.
A program may use at most 64 MiB of HBM per device.

v0:
```python
import jax
import jax.numpy as jnp
from jax import lax
from jax.sharding import PartitionSpec as P

DAMP = 0.5


def split_stats(flat, wide, narrow):
    count = flat.shape[0]
    wpart = flat[:, : wide * wide].reshape(count, wide, wide)
    npart = flat[:, wide * wide : wide * wide + narrow * narrow].reshape(count, narrow, narrow)
    mpart = flat[:, wide * wide + narrow * narrow :].reshape(count, narrow, wide)
    return (wpart, npart, mpart)


def damped_factor(cov):
    size = cov.shape[-1]
    return jax.vmap(jnp.linalg.cholesky)(cov + DAMP * jnp.eye(size, dtype=jnp.float32))


def solve_many(factors, rhs):
    return jax.vmap(lambda c, b: jax.scipy.linalg.cho_solve((c, True), b))(factors, rhs)


def on_device(wide_rows, narrow_rows, owner_map):
    layers, rows, wide = wide_rows.shape
    narrow = narrow_rows.shape[2]
    n_dp = lax.axis_size("dp")
    n_own = lax.axis_size("own")
    per_owner = layers // n_own + 1
    total = rows * n_dp * n_own
    wcov = (
        jnp.einsum("lrw,lrv->lwv", wide_rows, wide_rows, preferred_element_type=jnp.float32) / total
    )
    ncov = (
        jnp.einsum("lrn,lrm->lnm", narrow_rows, narrow_rows, preferred_element_type=jnp.float32)
        / total
    )
    mixed = (
        jnp.einsum("lrn,lrw->lnw", narrow_rows, wide_rows, preferred_element_type=jnp.float32)
        / total
    )
    flat = jnp.concatenate(
        [wcov.reshape(layers, -1), ncov.reshape(layers, -1), mixed.reshape(layers, -1)], axis=1
    )
    same = owner_map[:, None] == owner_map[None, :]
    order = jnp.arange(layers, dtype=jnp.int32)
    earlier = order[None, :] < order[:, None]
    rank = jnp.sum((same & earlier).astype(jnp.int32), axis=1)
    slot = owner_map * per_owner + rank
    slot_count = n_own * per_owner
    slot_table = (slot[:, None] == jnp.arange(slot_count, dtype=jnp.int32)[None, :]).astype(
        jnp.float32
    )
    col_width = wide // n_dp
    row_width = narrow // n_own
    dp_index = lax.axis_index("dp")
    own_index = lax.axis_index("own")
    pick_cols = lax.dynamic_slice_in_dim(
        jnp.eye(wide, dtype=jnp.float32), dp_index * col_width, col_width, 1
    )
    summed = lax.psum(flat, ("dp", "own"))
    wpart, npart, mpart = split_stats(summed, wide, narrow)
    inverse_cols = solve_many(
        damped_factor(wpart), jnp.broadcast_to(pick_cols, (layers, wide, col_width))
    )
    own_table = lax.dynamic_slice_in_dim(slot_table, own_index * per_owner, per_owner, 1)
    filled = jnp.sum(own_table, axis=0)
    kept = jnp.einsum("lc,lwk->cwk", own_table, inverse_cols, precision=lax.Precision.HIGHEST)
    kept = kept + (1.0 - filled)[:, None, None] * pick_cols[None, :, :] / DAMP
    pick_rows = lax.dynamic_slice_in_dim(
        jnp.eye(narrow, dtype=jnp.float32), own_index * row_width, row_width, 1
    )
    narrow_inv = solve_many(
        damped_factor(npart), jnp.broadcast_to(pick_rows, (layers, narrow, row_width))
    )
    inner = jnp.einsum("lnw,lwk->lnk", mpart, inverse_cols, precision=lax.Precision.HIGHEST)
    update = jnp.einsum("lnr,lnk->lrk", narrow_inv, inner, precision=lax.Precision.HIGHEST)
    return (kept, update)


def solution(mesh):
    in_specs = (P(None, ("dp", "own"), None), P(None, ("dp", "own"), None), P())
    out_specs = (P("own", None, "dp"), P(None, "own", "dp"))
    return jax.shard_map(
        on_device, mesh=mesh, in_specs=in_specs, out_specs=out_specs, check_vma=False
    )
```

profile of v0, /device:TPU:1, one launch (start us, length us, event | category | flops | bytes accessed | tf_op | source)
XLA Modules:
  0.0 982.7 jit_solution(11567906198939338761)
XLA Ops:
  7.2 2.6 fusion.2
  10.5 0.8 fusion.1
  11.2 1.1 multiply_bitcast_fusion
  12.7 0.6 copy.76
  13.3 1.2 copy.74
  14.5 2.1 pad_maximum_fusion
  16.8 0.7 copy.53
  20.2 286.0 %all-reduce.3.cloned.1.call-done = f32[8,114688]{1,0:T(8,128)} async-done(((f32[8,114688]{1,0:T(8,128)}), f32[8,114688]{1,0:T(8,128)}) %all-reduce.3.cloned.1.call-update) | async-done | bytes 3670032 | tf_op jit(solution)/shard_map/psum | solution.py:63
  306.1 1.1 slice_bitcast_fusion
  307.2 0.9 copy.90
  308.1 2.0 copy.51
  310.2 1.9 broadcast_add_fusion.1
  312.1 2.0 copy.52
  314.1 2.1 fusion.12
  316.2 95.2 %custom-call.35 = f32[8,128,128]{2,1,0:T(8,128)} custom-call(f32[8,128,128]{2,1,0:T(8,128)} %fusion.12), custom_call_target="Cholesky" | custom-call | tf_op jit(solution)/shard_map/vmap(jit(cholesky))/cholesky | solution.py:19
  411.4 1.6 slice-done
  413.0 2.0 copy.89
  414.9 2.9 copy.40
  417.9 3.2 broadcast_add_fusion
  421.0 2.9 copy.41
  423.9 2.5 fusion
  426.4 1.3 copy-done.2
  427.8 0.9 cholesky.185
  428.6 95.3 %custom-call.31 = f32[8,128,128]{2,1,0:T(8,128)} custom-call(f32[8,128,128]{2,1,0:T(8,128)} %cholesky.185), custom_call_target="Cholesky" | custom-call | tf_op jit(solution)/shard_map/vmap(jit(cholesky))/cholesky | solution.py:19
  523.9 1.9 select_bitcast_fusion.1
  525.8 80.0 %custom-call.32 = f32[8,1,128,128]{2,3,1,0:T(8,128)} custom-call(f32[8,1,128,128]{3,2,1,0:T(8,128)} %select_bitcast_fusion.1), custom_call_target="InvertDiagBlocksLowerTriangular" | custom-call | tf_op jit(solution)/shard_map/vmap(jit(cholesky))/cholesky | solution.py:19
  605.8 2.7 cholesky.173
  608.5 1.4 constant_dynamic-update-slice_fusion.1
  610.0 2.0 convolution_subtract_fusion
  612.0 95.2 %custom-call.33 = f32[8,128,128]{2,1,0:T(8,128)} custom-call(f32[8,128,128]{2,1,0:T(8,128)} %convolution_subtract_fusion), custom_call_target="Cholesky" | custom-call | tf_op jit(solution)/shard_map/vmap(jit(cholesky))/cholesky | solution.py:19
  707.3 2.4 select_reduce_fusion
  709.8 1.0 select_bitcast_fusion
  710.7 80.0 %custom-call.36 = f32[8,1,128,128]{2,3,1,0:T(8,128)} custom-call(f32[8,1,128,128]{3,2,1,0:T(8,128)} %select_bitcast_fusion), custom_call_target="InvertDiagBlocksLowerTriangular" | custom-call | tf_op jit(solution)/shard_map/vmap(jit(_cho_solve))/triangular_solve | solution.py:23
  790.9 3.2 select_select_fusion
  794.2 8.0 while.1
  794.8 3.5 bitcast_dynamic-update-slice_fusion.2
  798.9 3.3 bitcast_dynamic-update-slice_fusion.2
  802.2 158.6 %custom-call.34 = f32[8,2,128,128]{2,3,1,0:T(8,128)} custom-call(f32[8,2,128,128]{3,2,1,0:T(8,128)} %bitcast.95), custom_call_target="InvertDiagBlocksLowerTriangular" | custom-call | tf_op jit(solution)/shard_map/vmap(jit(_cho_solve))/triangular_solve | solution.py:23
  960.9 1.7 fusion.15
  962.6 2.0 convolution_subtract_fusion.2
  964.5 1.7 fusion.17
  966.2 2.0 fusion.16
  968.2 1.7 convolution_subtract_fusion.1
  969.9 0.9 fusion.14
  970.9 1.2 fusion.3
  972.1 0.8 convolution_add_fusion
  974.1 0.9 fusion.8
  975.0 0.8 fusion.27
  (71 shorter events, 6.5 us)
Async XLA Ops:
  7.2 2.8 copy-start
  7.2 299.0 %all-reduce.3.cloned.1.call-start = ((), (), s32[]{:S(2)}) async-start(), calls=%async_computation | async-start | bytes 7340032 | tf_op jit(solution)/shard_map/psum | solution.py:63
  7.2 3.3 copy-start.1
  16.6 1.0 copy-start.16
  16.6 2.3 copy-start.8
  17.7 0.5 copy-start.15
  18.9 0.6 copy-start.11
  411.4 1.6 slice-start
  426.4 1.3 copy-start.2
  605.8 2.7 copy-start.3
  605.8 2.7 copy-start.7
  608.5 98.7 %copy-start.9 = (pred[128,128]{1,0:T(8,128)(4,1)S(1)}, pred[128,128]{1,0:T(8,128)(4,1)}, u32[]{:S(2)}) copy-start(pred[128,128]{1,0:T(8,128)(4,1)} %copy-done.8) | copy-start | bytes 49156
  707.3 2.5 copy-start.6
  790.9 3.3 copy-start.17
  794.2 166.6 %copy-start.14 = (f32[128,4]{0,1:T(4,128)S(1)}, f32[128,4]{0,1:T(4,128)}, u32[]{:S(2)}) copy-start(f32[128,4]{0,1:T(4,128)} %get-tuple-element.31) | copy-start | bytes 6148
  794.2 168.3 %copy-start.13 = (f32[128,4]{0,1:T(4,128)S(1)}, f32[128,4]{0,1:T(4,128)}, u32[]{:S(2)}) copy-start(f32[128,4]{0,1:T(4,128)} %get-tuple-element.30) | copy-start | bytes 6148
  960.9 9.0 copy-start.4
  964.5 6.3 slice-start.1
  968.2 3.9 copy-start.12
  968.2 3.9 copy-start.18
  968.2 5.3 copy-start.5
  968.2 5.3 copy-start.10
Sparse Core Ops, SparseCore 0:
  16.7 289.3 all-reduce.2
where the time goes:
time: 984 us; the launch traced here: 983 us
  other arithmetic  627 us (64%)
  waiting for transfers between devices  286 us (29%)
  local copies, waits for them, and re-layouts  33.5 us (3%)
  matrix products  22.2 us (2%)
  between operations  14.3 us (1%)
    another operation x11, other arithmetic, damped_factor(): jax.vmap(jnp.linalg.cholesky)(cov + DAMP * jnp.eye(size, dtype=jnp.float32))  370 us
    psum x1, waiting for transfers between devices, on_device(): summed = lax.psum(flat, ('dp', 'own'))  286 us
    another operation x7, other arithmetic, solve_many(): jax.scipy.linalg.cho_solve((c, True), b)  244 us
  transfers between devices with their start and end apart: 1, of which 1 were waited for; matrix products, arithmetic and copies ran while one was open for 0% of the time, Pallas kernels for 0%

commit v1 on v0

v1 whole, which is shorter than its diff:
```python
import functools

import jax
import jax.numpy as jnp
from jax import lax
from jax.experimental import pallas as pl
from jax.experimental.pallas import tpu as pltpu
from jax.sharding import PartitionSpec as P

DAMP = 0.5
MESH = pl.DeviceIdType.MESH
HI = lax.Precision.HIGHEST
f32, bf16 = jnp.float32, jnp.bfloat16
LAYERS, ROWS, WIDE, NARROW = 8, 768, 256, 128
NZ, NY, NO = 8, 4, 8
HALF = 384
ZROWS = HALF // NZ


def place():
    dp = lax.axis_index("dp")
    return dp, lax.axis_index("own"), dp // 8, lax.rem(dp // 2, 4), lax.rem(dp, 2)


def remote(src, dst, send, recv, dp, own):
    return pltpu.make_async_remote_copy(
        src_ref=src, dst_ref=dst, send_sem=send, recv_sem=recv,
        device_id=(dp, own), device_id_type=MESH,
    )


def gram(a, b):
    return lax.dot_general(a, b, (((0,), (0,)), ((), ())), preferred_element_type=f32)


def sum_kernel(
    wide_hbm, narrow_hbm, out_ref, wbuf, nbuf, part, core_rx, own_rx, z_rx, y_rx, z_tx, y_tx,
    in_sem, s0, r0, s1, r1, s2, r2, s3, r3, s4, r4, s5, r5,
):
    dp, own, z, yh, core = place()
    sib = dp + 1 - 2 * core

    def layer_of(t):
        return lax.rem(own + 1 + t, LAYERS)

    def loads(t):
        l = layer_of(t)
        return (
            pltpu.make_async_copy(wide_hbm.at[l], wbuf.at[t], in_sem.at[0, t]),
            pltpu.make_async_copy(narrow_hbm.at[l], nbuf.at[t], in_sem.at[1, t]),
        )

    for t in range(LAYERS):
        for copy in loads(t):
            copy.start()

    def z_peer(i):
        zz = lax.rem(z + i, NZ)
        return zz, zz * 8 + yh * 2 + core

    def y_peer(i):
        yy = lax.rem(yh + i, NY)
        return yy, z * 8 + yy * 2 + core

    def own_peer(i):
        return lax.rem(own + i, NO)

    barrier = pltpu.get_barrier_semaphore()
    pl.semaphore_signal(barrier, inc=1, device_id=(sib, own), device_id_type=MESH)
    for i in range(1, NO):
        pl.semaphore_signal(barrier, inc=1, device_id=(dp, own_peer(i)), device_id_type=MESH)
    for i in range(1, NZ):
        pl.semaphore_signal(barrier, inc=1, device_id=(z_peer(i)[1], own), device_id_type=MESH)
    for i in range(1, NY):
        pl.semaphore_signal(barrier, inc=1, device_id=(y_peer(i)[1], own), device_id_type=MESH)

    def core_copy(t):
        return remote(part.at[t, 1 - core], core_rx.at[t], s0.at[t], r0.at[t], sib, own)

    def own_copy(t):
        return remote(part.at[t, core], own_rx.at[t], s1.at[t], r1.at[t], dp, layer_of(t))

    def stats(t):
        for copy in loads(t):
            copy.wait()
        wide, narrow = wbuf[t], nbuf[t]
        left, right = wide[:, :128], wide[:, 128:]
        top = gram(left, wide)
        part[t, 0, 0:128, :] = top[:, :128]
        part[t, 0, 128:256, :] = top[:, 128:]
        part[t, 0, 256:384, :] = gram(right, right)
        part[t, 1, 0:128, :] = gram(narrow, narrow)
        mixed = gram(narrow, wide)
        part[t, 1, 128:256, :] = mixed[:, :128]
        part[t, 1, 256:384, :] = mixed[:, 128:]

    def pass_on(t):
        core_copy(t).wait_recv()
        part[t, core] = part[t, core] + core_rx[t]

    stats(0)
    pl.semaphore_wait(barrier, 1 + (NO - 1) + (NZ - 1) + (NY - 1))
    core_copy(0).start()

    @pl.loop(1, LAYERS)
    def _(t):
        stats(t)
        core_copy(t).start()
        pass_on(t - 1)
        own_copy(t - 1).start()

    pass_on(LAYERS - 1)
    for t in range(LAYERS - 1):
        own_copy(t).wait_recv()
    total = part[LAYERS - 1, core]
    for t in range(LAYERS - 1):
        total = total + own_rx[t]
    z_tx[...] = total.reshape(NZ, ZROWS, 128)

    def z_copy(i):
        zz, peer = z_peer(i)
        return remote(z_tx.at[zz], z_rx.at[i], s2.at[i], r2.at[i], peer, own)

    for i in range(1, NZ):
        z_copy(i).start()
    acc = z_tx[z]
    for i in range(1, NZ):
        z_copy(i).wait_recv()
        acc = acc + z_rx[i]
    y_tx[...] = acc

    def y_copy(i):
        return remote(y_tx, y_rx.at[i], s3.at[i], r3.at[i], y_peer(i)[1], own)

    for i in range(1, NY):
        y_copy(i).start()
    acc = y_tx[...]
    for i in range(1, NY):
        y_copy(i).wait_recv()
        acc = acc + y_rx[i]
    out_ref[core, z] = acc

    def gather_copy(i):
        return remote(out_ref.at[core, z], out_ref.at[core, z], s4.at[i], r4.at[i], z_peer(i)[1], own)

    def arrival(i):
        zz = lax.rem(z + NZ - i, NZ)
        return remote(out_ref.at[core, zz], out_ref.at[core, zz], s4.at[i], r4.at[i], z_peer(i)[1], own)

    def twin_copy(i):
        zz = lax.rem(z + NZ - i, NZ)
        return remote(out_ref.at[core, zz], out_ref.at[core, zz], s5.at[i], r5.at[i], sib, own)

    def twin_arrival(i):
        zz = lax.rem(z + NZ - i, NZ)
        return remote(out_ref.at[1 - core, zz], out_ref.at[1 - core, zz], s5.at[i], r5.at[i], sib, own)

    for i in range(1, NZ):
        gather_copy(i).start()
    twin_copy(0).start()
    for i in range(1, NZ):
        arrival(i).wait_recv()
        twin_copy(i).start()
    for i in range(NZ):
        twin_arrival(i).wait_recv()

    for t in range(LAYERS):
        core_copy(t).wait_send()
    for t in range(LAYERS - 1):
        own_copy(t).wait_send()
    for i in range(1, NZ):
        z_copy(i).wait_send()
    for i in range(1, NY):
        y_copy(i).wait_send()
    for i in range(1, NZ):
        gather_copy(i).wait_send()
    for i in range(NZ):
        twin_copy(i).wait_send()


def summed_stats(wide_rows, narrow_rows):
    dma = pltpu.SemaphoreType.DMA
    return pl.pallas_call(
        sum_kernel,
        out_shape=jax.ShapeDtypeStruct((2, NZ, ZROWS, 128), f32),
        in_specs=[pl.BlockSpec(memory_space=pl.ANY)] * 2,
        out_specs=pl.BlockSpec(memory_space=pltpu.VMEM),
        scratch_shapes=[
            pltpu.VMEM((LAYERS, ROWS, WIDE), bf16),
            pltpu.VMEM((LAYERS, ROWS, NARROW), bf16),
            pltpu.VMEM((LAYERS, 2, HALF, 128), f32),
            pltpu.VMEM((LAYERS, HALF, 128), f32),
            pltpu.VMEM((LAYERS - 1, HALF, 128), f32),
            pltpu.VMEM((NZ, ZROWS, 128), f32),
            pltpu.VMEM((NY, ZROWS, 128), f32),
            pltpu.VMEM((NZ, ZROWS, 128), f32),
            pltpu.VMEM((ZROWS, 128), f32),
            dma((2, LAYERS)), dma((LAYERS,)), dma((LAYERS,)), dma((LAYERS,)), dma((LAYERS,)),
            dma((NZ,)), dma((NZ,)), dma((NY,)), dma((NY,)),
            dma((NZ,)), dma((NZ,)), dma((NZ,)), dma((NZ,)),
        ],
        compiler_params=pltpu.CompilerParams(
            collective_id=0, has_side_effects=True, vmem_limit_bytes=40 << 20
        ),
    )(wide_rows, narrow_rows)


def split3(x):
    a = x.astype(bf16)
    r = x - a.astype(f32)
    b = r.astype(bf16)
    r = r - b.astype(f32)
    return a, b, r.astype(bf16)


def outer(p, r):
    p1, p2, p3 = split3(p)
    r1, r2, r3 = split3(r)
    lhs = jnp.concatenate([p1, p1, p2, p2, p1, p3], 0)
    rhs = jnp.concatenate([r1, r2, r1, r2, r3, r1], 0)
    return lax.dot_general(lhs, rhs, (((0,), (0,)), ((), ())), preferred_element_type=f32)


def sweep_panel(a_ref, k, n):
    lo = 8 * k
    sub = lax.broadcasted_iota(jnp.int32, (8, 128), 0)
    lane = lax.broadcasted_iota(jnp.int32, (8, 128), 1)
    rows = a_ref[lo : lo + 8, :]
    chunks = [rows[:, 128 * c : 128 * c + 128] for c in range(n // 128)]
    kc, kl = lo // 128, lo % 128
    cols = [jnp.broadcast_to(chunks[kc][:, kl + j : kl + j + 1], (8, 128)) for j in range(8)]
    for p in range(8):
        rec = 1.0 / jnp.broadcast_to(cols[p][p : p + 1, :], (8, 128))
        factor = cols[p]
        here = sub == p
        unit = jnp.where(here, 1.0, 0.0)
        chunks[kc] = jnp.where(lane == kl + p, unit, chunks[kc])

        def step(x):
            row = jnp.broadcast_to(x[p : p + 1, :], (8, 128)) * rec
            return jnp.where(here, row, x - factor * row)

        chunks = [step(x) for x in chunks]
        cols = [step(cols[j]) if j > p else cols[j] for j in range(8)]
    inside = (lane >= kl) & (lane < kl + 8)
    chunks[kc] = jnp.where(inside, -chunks[kc], chunks[kc])
    swept = jnp.concatenate(chunks, 1) if len(chunks) > 1 else chunks[0]
    change = outer(rows, swept)
    lanes = lax.broadcasted_iota(jnp.int32, (1, n), 1)
    own_cols = (lanes >= lo) & (lanes < lo + 8)
    a_ref[...] = jnp.where(own_cols, 0.0, a_ref[...]) - change
    a_ref[lo : lo + 8, :] = swept


def eye(n):
    i = lax.broadcasted_iota(jnp.int32, (n, n), 0)
    j = lax.broadcasted_iota(jnp.int32, (n, n), 1)
    return jnp.where(i == j, 1.0, 0.0).astype(f32)


def inverse_kernel(total, s_ref, out_ref, a_ref, n_ref):
    dp = lax.axis_index("dp")
    damp = DAMP * eye(128)
    cross = s_ref[128:256, :] / total
    a_ref[0:128, 0:128] = s_ref[0:128, :] / total + damp
    a_ref[0:128, 128:256] = cross
    a_ref[128:256, 0:128] = cross.T
    a_ref[128:256, 128:256] = s_ref[256:384, :] / total + damp
    n_ref[...] = s_ref[384:512, :] / total + damp
    for k in range(WIDE // 8):
        sweep_panel(a_ref, k, WIDE)
        if k < NARROW // 8:
            sweep_panel(n_ref, k, NARROW)
    x = -a_ref[pl.ds(pl.multiple_of(dp // 2 * 8, 8), 8), :]
    last = (((1,), (1,)), ((), ()))
    inner = lax.dot_general(x[:, :128], s_ref[512:640, :] / total, last, precision=HI, preferred_element_type=f32)
    inner = inner + lax.dot_general(x[:, 128:], s_ref[640:768, :] / total, last, precision=HI, preferred_element_type=f32)
    u = -jnp.dot(inner, n_ref[...], precision=HI, preferred_element_type=f32)
    both = jnp.concatenate([x, u], 1)
    out_ref[...] = jnp.where(lax.rem(dp, 2) == 0, both[0:4], both[4:8])


def inverse_columns(stats, total):
    return pl.pallas_call(
        functools.partial(inverse_kernel, float(total)),
        out_shape=jax.ShapeDtypeStruct((4, WIDE + NARROW), f32),
        in_specs=[pl.BlockSpec(memory_space=pltpu.VMEM)],
        out_specs=pl.BlockSpec(memory_space=pltpu.VMEM),
        scratch_shapes=[pltpu.VMEM((WIDE, WIDE), f32), pltpu.VMEM((NARROW, NARROW), f32)],
    )(stats)


def exchange_kernel(cols_ref, table_ref, kept_ref, update_ref, rx, send, recv):
    dp, own, _, _, _ = place()

    def peer(i):
        return lax.rem(own + i, NO)

    barrier = pltpu.get_barrier_semaphore()
    for i in range(1, NO):
        pl.semaphore_signal(barrier, inc=1, device_id=(dp, peer(i)), device_id_type=MESH)
    pl.semaphore_wait(barrier, NO - 1)

    def copy(i):
        return remote(cols_ref, rx.at[own], send.at[i], recv.at[i], dp, peer(i))

    def arrival(i):
        return remote(cols_ref, rx.at[lax.rem(own + NO - i, NO)], send.at[i], recv.at[i], dp, peer(i))

    for i in range(1, NO):
        copy(i).start()
    rx[own] = cols_ref[...]
    i0 = lax.broadcasted_iota(jnp.int32, (4, WIDE), 0)
    i1 = lax.broadcasted_iota(jnp.int32, (4, WIDE), 1)
    empty = jnp.where(i1 == dp * 4 + i0, 1.0 / DAMP, 0.0).astype(f32)
    for i in range(1, NO):
        arrival(i).wait_recv()
    kept = [empty, empty]
    shift = lax.rem(128 - 16 * own, 128)
    for l in range(LAYERS):
        got = rx[l]
        for c in range(2):
            hit = jnp.broadcast_to(table_ref[c, l : l + 1, 0:1], (4, WIDE)) > 0.5
            kept[c] = jnp.where(hit, got[:, :WIDE], kept[c])
        part = jnp.concatenate([got[:, WIDE:], got[:, WIDE:]], 0)
        update_ref[l] = pltpu.roll(part, shift, 1)[0:4, 0:16]
    kept_ref[0] = kept[0]
    kept_ref[1] = kept[1]
    for i in range(1, NO):
        copy(i).wait_send()


def exchange(cols, table):
    dma = pltpu.SemaphoreType.DMA
    vmem = pl.BlockSpec(memory_space=pltpu.VMEM)
    return pl.pallas_call(
        exchange_kernel,
        out_shape=(
            jax.ShapeDtypeStruct((2, 4, WIDE), f32),
            jax.ShapeDtypeStruct((LAYERS, 4, 16), f32),
        ),
        in_specs=[vmem, vmem],
        out_specs=(vmem, vmem),
        scratch_shapes=[pltpu.VMEM((NO, 4, WIDE + NARROW), f32), dma((NO,)), dma((NO,))],
        compiler_params=pltpu.CompilerParams(collective_id=1, has_side_effects=True),
    )(cols, table)


def on_device(wide_rows, narrow_rows, owner_map):
    same = owner_map[:, None] == owner_map[None, :]
    order = jnp.arange(LAYERS, dtype=jnp.int32)
    rank = jnp.sum((same & (order[None, :] < order[:, None])).astype(jnp.int32), axis=1)
    mine = lax.axis_index("own") * 2 + jnp.arange(2, dtype=jnp.int32)
    table = ((owner_map * 2 + rank)[None, :] == mine[:, None]).astype(f32)
    table = jnp.broadcast_to(table[:, :, None], (2, LAYERS, 128))
    stats = summed_stats(wide_rows, narrow_rows).reshape(768, 128)
    cols = inverse_columns(stats, ROWS * 512)
    kept, update = exchange(cols, table)
    return kept.transpose(0, 2, 1), update.transpose(0, 2, 1)


def solution(mesh):
    in_specs = (P(None, ("dp", "own"), None), P(None, ("dp", "own"), None), P())
    out_specs = (P("own", None, "dp"), P(None, "own", "dp"))
    return jax.shard_map(
        on_device, mesh=mesh, in_specs=in_specs, out_specs=out_specs, check_vma=False
    )
```

time: 984 us -> 96.6 us (0.10)
  other arithmetic: 627 us -> 0.26 us
  waiting for transfers between devices: 286 us -> 0 us
  Pallas kernels: 0 us -> 87.9 us
  local copies, waits for them, and re-layouts: 33.5 us -> 7.34 us
  matrix products: 22.2 us -> 0 us
  between operations: 14.3 us -> 0.67 us
    another operation x18 -> x0, other arithmetic: 614 us -> none  [the longest x11 370 us: damped_factor(): jax.vmap(jnp.linalg.cholesky)(cov + DAMP * jnp.eye(size, dtype=jnp.float32))]
    psum x1 -> x0, waiting for transfers between devices: 286 us -> none  [on_device(): summed = lax.psum(flat, ('dp', 'own'))]
    pallas_call x0 -> x3, Pallas kernels: none -> 87.9 us  [the longest x1 61.2 us: summed_stats(): pl.pallas_call(sum_kernel, out_shape=jax.ShapeDtypeStruct((2, NZ, ZROWS,...]
    another operation x10 -> x0, matrix products: 14.9 us -> none  [the longest x8 11.4 us: solve_many(): jax.scipy.linalg.cho_solve((c, True), b)]
    another operation x10 -> x0, local copies, waits for them, and re-layouts: 12.2 us -> none
  transfers between devices with their start and end apart: 1 -> 0, of which waited for: 1 -> 0; matrix products, arithmetic and copies ran while one was open for 0% -> 0% of each run, Pallas kernels for 0% -> 0%
where the time goes in v1:
time: 96.6 us; the launch traced here: 96.2 us
  Pallas kernels  87.9 us (91%)
  local copies, waits for them, and re-layouts  7.34 us (8%)
    pallas_call x1, Pallas kernels, summed_stats(): pl.pallas_call(sum_kernel, out_shape=jax.ShapeDtypeStruct((2, NZ, ZROWS,...  61.2 us
    pallas_call x1, Pallas kernels, inverse_columns(): pl.pallas_call(functools.partial(inverse_kernel, float(total)), out_shape...  13.9 us
    pallas_call x1, Pallas kernels, exchange(): pl.pallas_call(exchange_kernel, out_shape=(jax.ShapeDtypeStruct((2, 4, WI...  12.8 us
    unnamed x10, local copies, waits for them, and re-layouts  6.66 us

profile of v1, /device:TPU:1, one launch (start us, length us, event | category | flops | bytes accessed | tf_op | source)
XLA Modules:
  0.0 96.2 jit_solution(17363701722053990178)
XLA Ops:
  0.6 0.0 copy-start
  0.6 1.9 %copy-done = bf16[8,768,256]{2,1,0:T(8,128)(2,1)S(1)} copy-done((bf16[8,768,256]{2,1,0:T(8,128)(2,1)S(1)}, bf16[8,768,256]{2,1,0:T(8,128)(2,1)}, u32[]{:S(2)}) %copy-start) | copy-done | bytes 3145752
  2.5 0.0 copy-start.2
  2.5 1.4 %copy-done.2 = bf16[8,768,128]{2,1,0:T(8,128)(2,1)S(1)} copy-done((bf16[8,768,128]{2,1,0:T(8,128)(2,1)S(1)}, bf16[8,768,128]{2,1,0:T(8,128)(2,1)}, u32[]{:S(2)}) %copy-start.2) | copy-done | bytes 1572888
  3.9 0.0 copy-start.3
  3.9 61.2 %shard_map.50 = f32[2,8,48,128]{3,2,1,0:T(8,128)S(1)} custom-call(bf16[8,768,256]{2,1,0:T(8,128)(2,1)S(1)} %copy-done, bf16[8,768,128]{2,1,0:T(8,128)(2,1)S(1)} %copy-done.2), custom_call_target="tpu_custom_call" | custom-call | tf_op jit(solution)/shard_map/pallas_call | solution.py:183
  65.2 0.0 copy-start.1
  65.2 0.7 copy-done.1
  65.9 13.9 %shard_map.51.cols_ref = f32[4,384]{1,0:T(4,128)} custom-call(f32[768,128]{1,0:T(8,128)} %bitcast.3), custom_call_target="tpu_custom_call" | custom-call | tf_op jit(solution)/shard_map/pallas_call | solution.py:284
  79.9 0.0 copy-done.3
  79.9 0.2 convert_reduce_fusion
  80.1 0.1 compare_convert_fusion
  80.1 0.7 broadcast_in_dim.2.table_ref
  80.8 12.8 %shard_map.52 = (f32[2,4,256]{2,1,0:T(4,128)}, f32[8,4,16]{2,1,0:T(4,128)}) custom-call(f32[4,384]{1,0:T(4,128)} %shard_map.51.cols_ref, f32[2,8,128]{2,1,0:T(8,128)} %broadcast_in_dim.2.table_ref), custom_call_target="tpu_custom_call" | custom-call | tf_op jit(solution)/shard_map/pallas_call | solution.py:336
  93.6 1.3 %copy.7 = f32[2,256,4]{1,2,0:T(4,128)} copy(f32[2,256,4]{1,2,0:T(4,128)} %bitcast.5) | data formatting | bytes 16384
  94.9 1.3 %copy.8 = f32[8,16,4]{1,2,0:T(4,128)} copy(f32[8,16,4]{1,2,0:T(4,128)} %bitcast.4) | data formatting | bytes 4096
  (2 shorter events, 0.0 us)
Async XLA Ops:
  0.6 1.9 %copy-start = (bf16[8,768,256]{2,1,0:T(8,128)(2,1)S(1)}, bf16[8,768,256]{2,1,0:T(8,128)(2,1)}, u32[]{:S(2)}) copy-start(bf16[8,768,256]{2,1,0:T(8,128)(2,1)} %wide_hbm.1) | copy-start | bytes 9437188
  2.5 1.4 %copy-start.2 = (bf16[8,768,128]{2,1,0:T(8,128)(2,1)S(1)}, bf16[8,768,128]{2,1,0:T(8,128)(2,1)}, u32[]{:S(2)}) copy-start(bf16[8,768,128]{2,1,0:T(8,128)(2,1)} %narrow_hbm.1) | copy-start | bytes 4718596
  3.9 75.9 %copy-start.3 = (s32[8]{0:T(128)S(1)}, s32[8]{0:T(128)}, u32[]{:S(2)}) copy-start(s32[8]{0:T(128)} %param.5) | copy-start | bytes 100
  65.2 0.8 copy-start.1

commit v2 on v0

v2 whole, which is shorter than its diff:
```python
import functools

import jax
import jax.numpy as jnp
from jax import lax
from jax.experimental import pallas as pl
from jax.experimental.pallas import tpu as pltpu
from jax.sharding import PartitionSpec as P

DAMP = 0.5
MESH = pl.DeviceIdType.MESH
HI = lax.Precision.HIGHEST
f32, bf16 = jnp.float32, jnp.bfloat16
LAYERS, ROWS, WIDE, NARROW = 8, 768, 256, 128
NZ, NY, NO = 8, 4, 8


def place():
    dp = lax.axis_index("dp")
    return dp, lax.axis_index("own"), dp // 8, lax.rem(dp // 2, 4), lax.rem(dp, 2)


def remote(src, dst, send, recv, dp, own):
    return pltpu.make_async_remote_copy(
        src_ref=src, dst_ref=dst, send_sem=send, recv_sem=recv,
        device_id=(dp, own), device_id_type=MESH,
    )


def gram(a, b):
    return lax.dot_general(a, b, (((0,), (0,)), ((), ())), preferred_element_type=f32)


class Stream:
    def __init__(self, refs):
        (self.part, self.core_rx, self.own_rx, self.z_tx, self.z_rx, self.y_tx, self.y_rx, self.fin,
         self.sems, self.sems_y) = refs
        self.dp, self.own, self.z, self.yh, self.core = place()
        self.sib = self.dp + 1 - 2 * self.core

    @staticmethod
    def scratch(rows):
        vmem, dma = pltpu.VMEM, pltpu.SemaphoreType.DMA
        return [
            vmem((LAYERS, 2, rows, 128), f32), vmem((LAYERS, rows, 128), f32),
            vmem((LAYERS - 1, rows, 128), f32), vmem((NZ, rows // NZ, 128), f32),
            vmem((NZ, rows // NZ, 128), f32), vmem((rows // NZ, 128), f32),
            vmem((NY, rows // NZ, 128), f32), vmem((2, NZ, rows // NZ, 128), f32),
            dma((5, 2, 8)), dma((2, NY)),
        ]

    def to(self, src, dst, phase, i, dp, own):
        return remote(src, dst, self.sems.at[phase, 0, i], self.sems.at[phase, 1, i], dp, own)

    def layer_of(self, t):
        return lax.rem(self.own + 1 + t, LAYERS)

    def z_peer(self, i):
        zz = lax.rem(self.z + i, NZ)
        return zz, zz * 8 + self.yh * 2 + self.core

    def y_peer(self, i):
        return self.z * 8 + lax.rem(self.yh + i, NY) * 2 + self.core

    def core_copy(self, t):
        return self.to(self.part.at[t, 1 - self.core], self.core_rx.at[t], 0, t, self.sib, self.own)

    def own_copy(self, t):
        return self.to(self.part.at[t, self.core], self.own_rx.at[t], 1, t, self.dp, self.layer_of(t))

    def pass_on(self, t):
        self.core_copy(t).wait_recv()
        self.part[t, self.core] = self.part[t, self.core] + self.core_rx[t]

    def z_copy(self, i):
        zz, peer = self.z_peer(i)
        return self.to(self.z_tx.at[zz], self.z_rx.at[i], 2, i, peer, self.own)

    def y_copy(self, i):
        return remote(self.y_tx, self.y_rx.at[i], self.sems_y.at[0, i], self.sems_y.at[1, i], self.y_peer(i), self.own)

    def gather_copy(self, i):
        block = self.fin.at[self.core, self.z]
        return self.to(block, block, 3, i, self.z_peer(i)[1], self.own)

    def from_z(self, core, i):
        return self.fin.at[core, lax.rem(self.z + NZ - i, NZ)]

    def arrival(self, i):
        block = self.from_z(self.core, i)
        return self.to(block, block, 3, i, self.z_peer(i)[1], self.own)

    def twin_copy(self, i):
        block = self.from_z(self.core, i)
        return self.to(block, block, 4, i, self.sib, self.own)

    def twin_arrival(self, i):
        block = self.from_z(1 - self.core, i)
        return self.to(block, block, 4, i, self.sib, self.own)

    def own_done(self):
        total = self.part[LAYERS - 1, self.core]
        for t in range(LAYERS - 1):
            self.own_copy(t).wait_recv()
            total = total + self.own_rx[t]
        self.z_tx[...] = total.reshape(self.z_tx.shape)
        for i in range(1, NZ):
            self.z_copy(i).start()

    def z_done(self):
        acc = self.z_tx[self.z]
        for i in range(1, NZ):
            self.z_copy(i).wait_recv()
            acc = acc + self.z_rx[i]
        self.y_tx[...] = acc
        for i in range(1, NY):
            self.y_copy(i).start()

    def y_done(self):
        acc = self.y_tx[...]
        for i in range(1, NY):
            self.y_copy(i).wait_recv()
            acc = acc + self.y_rx[i]
        self.fin[self.core, self.z] = acc
        for i in range(1, NZ):
            self.gather_copy(i).start()
        self.twin_copy(0).start()

    def gather_done(self):
        for i in range(1, NZ):
            self.arrival(i).wait_recv()
            self.twin_copy(i).start()

    def twin_done(self):
        for i in range(NZ):
            self.twin_arrival(i).wait_recv()

    def drain(self):
        for t in range(LAYERS):
            self.core_copy(t).wait_send()
        for t in range(LAYERS - 1):
            self.own_copy(t).wait_send()
        for i in range(1, NZ):
            self.z_copy(i).wait_send()
            self.gather_copy(i).wait_send()
        for i in range(1, NY):
            self.y_copy(i).wait_send()
        for i in range(NZ):
            self.twin_copy(i).wait_send()


def split3(x):
    a = x.astype(bf16)
    r = x - a.astype(f32)
    b = r.astype(bf16)
    r = r - b.astype(f32)
    return a, b, r.astype(bf16)


def outer(p, r):
    p1, p2, p3 = split3(p)
    r1, r2, r3 = split3(r)
    lhs = jnp.concatenate([p1, p1, p2, p2, p1, p3], 0)
    rhs = jnp.concatenate([r1, r2, r1, r2, r3, r1], 0)
    return lax.dot_general(lhs, rhs, (((0,), (0,)), ((), ())), preferred_element_type=f32)


def sweep_panel(a_ref, k, n):
    lo = 8 * k
    sub = lax.broadcasted_iota(jnp.int32, (8, 128), 0)
    lane = lax.broadcasted_iota(jnp.int32, (8, 128), 1)
    rows = a_ref[lo : lo + 8, :]
    chunks = [rows[:, 128 * c : 128 * c + 128] for c in range(n // 128)]
    kc, kl = lo // 128, lo % 128
    cols = [jnp.broadcast_to(chunks[kc][:, kl + j : kl + j + 1], (8, 128)) for j in range(8)]
    for p in range(8):
        rec = 1.0 / jnp.broadcast_to(cols[p][p : p + 1, :], (8, 128))
        factor = cols[p]
        here = sub == p
        unit = jnp.where(here, 1.0, 0.0)
        chunks[kc] = jnp.where(lane == kl + p, unit, chunks[kc])

        def step(x):
            row = jnp.broadcast_to(x[p : p + 1, :], (8, 128)) * rec
            return jnp.where(here, row, x - factor * row)

        chunks = [step(x) for x in chunks]
        cols = [step(cols[j]) if j > p else cols[j] for j in range(8)]
    inside = (lane >= kl) & (lane < kl + 8)
    chunks[kc] = jnp.where(inside, -chunks[kc], chunks[kc])
    swept = jnp.concatenate(chunks, 1) if len(chunks) > 1 else chunks[0]
    change = outer(rows, swept)
    lanes = lax.broadcasted_iota(jnp.int32, (1, n), 1)
    own_cols = (lanes >= lo) & (lanes < lo + 8)
    a_ref[...] = jnp.where(own_cols, 0.0, a_ref[...]) - change
    a_ref[lo : lo + 8, :] = swept


def eye(n):
    i = lax.broadcasted_iota(jnp.int32, (n, n), 0)
    j = lax.broadcasted_iota(jnp.int32, (n, n), 1)
    return jnp.where(i == j, 1.0, 0.0).astype(f32)


def main_kernel(scale, wide_hbm, narrow_hbm, out_ref, wbuf, nbuf, in_sem, a_ref, n_ref, cols_ref, x_sem, *refs):
    first, second = Stream(refs[:10]), Stream(refs[10:])
    dp, own, z, yh, core = place()

    def loads(t):
        l = first.layer_of(t)
        return (
            pltpu.make_async_copy(wide_hbm.at[l], wbuf.at[t], in_sem.at[0, t]),
            pltpu.make_async_copy(narrow_hbm.at[l], nbuf.at[t], in_sem.at[1, t]),
        )

    for t in range(LAYERS):
        for copy in loads(t):
            copy.start()

    def own_peer(i):
        return lax.rem(own + i, NO)

    barrier = pltpu.get_barrier_semaphore()

    def greet(dp, own):
        pl.semaphore_signal(barrier, inc=1, device_id=(dp, own), device_id_type=MESH)

    greet(first.sib, own)
    for i in range(1, NO):
        greet(dp, own_peer(i))
    for i in range(1, NZ):
        greet(first.z_peer(i)[1], own)
    for i in range(1, NY):
        greet(first.y_peer(i), own)

    def stats_first(t):
        for copy in loads(t):
            copy.wait()
        wide, narrow = wbuf[t], nbuf[t]
        right = wide[:, 128:]
        top = gram(wide[:, :128], wide)
        first.part[t, 0, 0:128, :] = top[:, :128]
        first.part[t, 0, 128:256, :] = top[:, 128:]
        first.part[t, 1, 0:128, :] = gram(right, right)
        first.part[t, 1, 128:256, :] = gram(narrow, narrow)

    def stats_second(t):
        mixed = gram(nbuf[t], wbuf[t])
        second.part[t, 0] = mixed[:, :128]
        second.part[t, 1] = mixed[:, 128:]

    stats_first(0)
    pl.semaphore_wait(barrier, 1 + (NO - 1) + (NZ - 1) + (NY - 1))
    first.core_copy(0).start()

    @pl.loop(1, LAYERS)
    def _(t):
        stats_first(t)
        first.core_copy(t).start()
        first.pass_on(t - 1)
        first.own_copy(t - 1).start()

    stats_second(0)
    second.core_copy(0).start()
    first.pass_on(LAYERS - 1)

    @pl.loop(1, LAYERS)
    def _(t):
        stats_second(t)
        second.core_copy(t).start()
        second.pass_on(t - 1)
        second.own_copy(t - 1).start()

    second.pass_on(LAYERS - 1)
    first.own_done()
    first.z_done()
    first.y_done()
    first.gather_done()
    first.twin_done()
    second.own_done()

    damp = DAMP * eye(128)

    def block(b):
        return first.fin[b // 2, (b % 2) * 4 : (b % 2) * 4 + 4].reshape(128, 128) * scale

    cross = block(1)
    a_ref[0:128, 0:128] = block(0) + damp
    a_ref[0:128, 128:256] = cross
    a_ref[128:256, 0:128] = cross.T
    a_ref[128:256, 128:256] = block(2) + damp
    n_ref[...] = block(3) + damp
    between = {8: second.z_done, 16: second.y_done, 24: second.gather_done}
    for k in range(WIDE // 8):
        if k in between:
            between[k]()
        sweep_panel(a_ref, k, WIDE)
        if k < NARROW // 8:
            sweep_panel(n_ref, k, NARROW)
    second.twin_done()
    x = -a_ref[pl.ds(pl.multiple_of(dp // 2 * 8, 8), 8), :]
    last = (((1,), (1,)), ((), ()))
    inner = 0.0
    for b in range(2):
        half = second.fin[b].reshape(128, 128) * scale
        inner = inner + lax.dot_general(x[:, 128 * b : 128 * b + 128], half, last, precision=HI, preferred_element_type=f32)
    u = -jnp.dot(inner, n_ref[...], precision=HI, preferred_element_type=f32)
    both = jnp.concatenate([x, u], 1)
    cols_ref[...] = jnp.where(core == 0, both[0:4], both[4:8])

    def copy(i):
        return remote(cols_ref, out_ref.at[own], x_sem.at[0, i], x_sem.at[1, i], dp, own_peer(i))

    def arrival(i):
        return remote(cols_ref, out_ref.at[own_peer(NO - i)], x_sem.at[0, i], x_sem.at[1, i], dp, own_peer(i))

    for i in range(1, NO):
        copy(i).start()
    out_ref[own] = cols_ref[...]
    for i in range(1, NO):
        arrival(i).wait_recv()
    first.drain()
    second.drain()
    for i in range(1, NO):
        copy(i).wait_send()


def columns(wide_rows, narrow_rows, total):
    vmem, dma = pltpu.VMEM, pltpu.SemaphoreType.DMA
    return pl.pallas_call(
        functools.partial(main_kernel, 1.0 / total),
        out_shape=jax.ShapeDtypeStruct((NO, 4, WIDE + NARROW), f32),
        in_specs=[pl.BlockSpec(memory_space=pltpu.HBM)] * 2,
        out_specs=pl.BlockSpec(memory_space=pltpu.VMEM),
        scratch_shapes=[
            vmem((LAYERS, ROWS, WIDE), bf16), vmem((LAYERS, ROWS, NARROW), bf16), dma((2, LAYERS)),
            vmem((WIDE, WIDE), f32), vmem((NARROW, NARROW), f32), vmem((4, WIDE + NARROW), f32), dma((2, NO)),
            *Stream.scratch(256), *Stream.scratch(128),
        ],
        compiler_params=pltpu.CompilerParams(
            collective_id=0, has_side_effects=True, vmem_limit_bytes=60 << 20
        ),
    )(wide_rows, narrow_rows)


def select_kernel(owners, cols_ref, kept_ref, update_ref):
    dp, own, _, _, _ = place()
    i0 = lax.broadcasted_iota(jnp.int32, (4, WIDE), 0)
    i1 = lax.broadcasted_iota(jnp.int32, (4, WIDE), 1)
    empty = jnp.where(i1 == dp * 4 + i0, 1.0 / DAMP, 0.0).astype(f32)
    kept = [empty, empty]
    shift = lax.rem(128 - 16 * own, 128)
    for l in range(LAYERS):
        slot = owners[l] * 2
        for j in range(l):
            slot = slot + jnp.where(owners[j] == owners[l], 1, 0)
        got = cols_ref[l]
        kept = [jnp.where(slot == own * 2 + c, got[:, :WIDE], kept[c]) for c in range(2)]
        part = jnp.concatenate([got[:, WIDE:], got[:, WIDE:]], 0)
        update_ref[l] = pltpu.roll(part, shift, 1)[0:4, 0:16]
    kept_ref[0] = kept[0]
    kept_ref[1] = kept[1]


def select(owner_map, cols):
    vmem = pl.BlockSpec(memory_space=pltpu.VMEM)
    return pl.pallas_call(
        select_kernel,
        out_shape=(
            jax.ShapeDtypeStruct((2, 4, WIDE), f32),
            jax.ShapeDtypeStruct((LAYERS, 4, 16), f32),
        ),
        in_specs=[pl.BlockSpec(memory_space=pltpu.SMEM), vmem],
        out_specs=(vmem, vmem),
    )(owner_map, cols)


def on_device(wide_rows, narrow_rows, owner_map):
    cols = columns(wide_rows, narrow_rows, ROWS * 512)
    kept, update = select(owner_map, cols)
    return kept.transpose(0, 2, 1), update.transpose(0, 2, 1)


def solution(mesh):
    in_specs = (P(None, ("dp", "own"), None), P(None, ("dp", "own"), None), P())
    out_specs = (P("own", None, "dp"), P(None, "own", "dp"))
    return jax.shard_map(
        on_device, mesh=mesh, in_specs=in_specs, out_specs=out_specs, check_vma=False
    )
```

time: 984 us -> 80.1 us (0.08)
  other arithmetic: 627 us -> 0 us
  waiting for transfers between devices: 286 us -> 0 us
  Pallas kernels: 0 us -> 79 us
  local copies, waits for them, and re-layouts: 33.5 us -> 0 us
  matrix products: 22.2 us -> 0 us
  between operations: 14.3 us -> 0.64 us
    another operation x18 -> x0, other arithmetic: 614 us -> none  [the longest x11 370 us: damped_factor(): jax.vmap(jnp.linalg.cholesky)(cov + DAMP * jnp.eye(size, dtype=jnp.float32))]
    psum x1 -> x0, waiting for transfers between devices: 286 us -> none  [on_device(): summed = lax.psum(flat, ('dp', 'own'))]
    pallas_call x0 -> x2, Pallas kernels: none -> 79 us  [the longest x1 77.5 us: columns(): pl.pallas_call(functools.partial(main_kernel, 1.0 / total), out_shape=jax...]
    another operation x10 -> x0, matrix products: 14.9 us -> none  [the longest x8 11.4 us: solve_many(): jax.scipy.linalg.cho_solve((c, True), b)]
    another operation x10 -> x0, local copies, waits for them, and re-layouts: 12.2 us -> none
  transfers between devices with their start and end apart: 1 -> 0, of which waited for: 1 -> 0; matrix products, arithmetic and copies ran while one was open for 0% -> 0% of each run, Pallas kernels for 0% -> 0%
where the time goes in v2:
time: 80.1 us; the launch traced here: 79.6 us
  Pallas kernels  79 us (99%)
    pallas_call x1, Pallas kernels, columns(): pl.pallas_call(functools.partial(main_kernel, 1.0 / total), out_shape=jax...  77.5 us

profile of v2, /device:TPU:1, one launch (start us, length us, event | category | flops | bytes accessed | tf_op | source)
XLA Modules:
  0.0 79.6 jit_solution(17039959721237588936)
XLA Ops:
  0.6 77.5 %shard_map.50.cols_ref = f32[8,4,384]{2,1,0:T(4,128)} custom-call(bf16[8,768,256]{2,1,0:T(8,128)(2,1)} %wide_hbm.1, bf16[8,768,128]{2,1,0:T(8,128)(2,1)} %narrow_hbm.1), custom_call_target="tpu_custom_call" | custom-call | tf_op jit(solution)/shard_map/pallas_call | solution.py:330
  78.1 1.5 %shard_map.51 = (f32[2,4,256]{2,1,0:T(4,128)}, f32[8,4,16]{2,1,0:T(4,128)}) custom-call(s32[8]{0:T(128)} %owners.1, f32[8,4,384]{2,1,0:T(4,128)} %shard_map.50.cols_ref), custom_call_target="tpu_custom_call" | custom-call | tf_op jit(solution)/shard_map/pallas_call | solution.py:367

commit v3 on v2

v3 whole, which is shorter than its diff:
```python
import functools

import jax
import jax.numpy as jnp
from jax import lax
from jax.experimental import pallas as pl
from jax.experimental.pallas import tpu as pltpu
from jax.sharding import PartitionSpec as P

DAMP = 0.5
MESH = pl.DeviceIdType.MESH
HI = lax.Precision.HIGHEST
f32, bf16 = jnp.float32, jnp.bfloat16
LAYERS, ROWS, WIDE, NARROW = 8, 768, 256, 128
NZ, NY, NO = 8, 4, 8


def place():
    dp = lax.axis_index("dp")
    return dp, lax.axis_index("own"), dp // 8, lax.rem(dp // 2, 4), lax.rem(dp, 2)


def remote(src, dst, send, recv, dp, own):
    return pltpu.make_async_remote_copy(
        src_ref=src, dst_ref=dst, send_sem=send, recv_sem=recv,
        device_id=(dp, own), device_id_type=MESH,
    )


def gram(a, b):
    return lax.dot_general(a, b, (((0,), (0,)), ((), ())), preferred_element_type=f32)


R = 192
ZR = R // NZ
DX = (2, 2, 1, 1, 3, 3, 0, 0)


class Stream:
    def __init__(self, refs):
        (self.part, self.core_rx, self.relay_rx, self.x_rx, self.yl_rx, self.z_tx, self.z_rx, self.y_tx, self.y_rx,
         self.fin, self.sems, self.sems_y) = refs
        self.dp, self.own, self.z, self.yh, self.core = place()
        self.sib = self.dp + 1 - 2 * self.core
        self.x, self.yl = lax.rem(self.own, 4), self.own // 4

    @staticmethod
    def scratch():
        vmem, dma = pltpu.VMEM, pltpu.SemaphoreType.DMA
        return [
            vmem((LAYERS, 2, R, 128), f32), vmem((LAYERS, R, 128), f32), vmem((4, R // 2, 128), f32),
            vmem((4, R, 128), f32), vmem((R, 128), f32), vmem((NZ, ZR, 128), f32), vmem((NZ, ZR, 128), f32),
            vmem((ZR, 128), f32), vmem((NY, ZR, 128), f32), vmem((2, NZ, ZR, 128), f32),
            dma((6, 2, 8)), dma((2, NY)),
        ]

    def to(self, src, dst, phase, i, dp, own):
        return remote(src, dst, self.sems.at[phase, 0, i], self.sems.at[phase, 1, i], dp, own)

    def x_peer(self, d):
        return self.yl * 4 + lax.rem(self.x + d, 4)

    def yl_peer(self):
        return (1 - self.yl) * 4 + self.x

    def layer_of(self, t):
        return (self.yl if t % 2 else 1 - self.yl) * 4 + lax.rem(self.x + DX[t], 4)

    def z_peer(self, i):
        zz = lax.rem(self.z + i, NZ)
        return zz, zz * 8 + self.yh * 2 + self.core

    def y_peer(self, i):
        return self.z * 8 + lax.rem(self.yh + i, NY) * 2 + self.core

    def mine(self, t):
        return self.part.at[t, self.core]

    def core_copy(self, t):
        return self.to(self.part.at[t, 1 - self.core], self.core_rx.at[t], 0, t, self.sib, self.own)

    def relay(self, i):
        half = pl.ds(0, R // 2) if i < 2 else pl.ds(R // 2, R // 2)
        return self.to(
            self.part.at[i % 2, self.core, half], self.relay_rx.at[i], 1, i, self.dp, self.x_peer(1 if i < 2 else 3)
        )

    def x_copy(self, i):
        return self.to(self.mine(i + 2), self.x_rx.at[i], 2, i, self.dp, self.x_peer(1 if i < 2 else 3))

    def yl_copy(self):
        return self.to(self.mine(6), self.yl_rx, 2, 4, self.dp, self.yl_peer())

    def pass_on(self, t):
        self.core_copy(t).wait_recv()
        total = self.part[t, self.core] + self.core_rx[t]
        if t < 2:
            self.part[t, self.core] = total
            self.relay(t).start()
            self.relay(t + 2).start()
        elif t < 6:
            i = t - 2
            self.relay(i).wait_recv()
            lo = 0 if i < 2 else R // 2
            self.part[t, self.core] = total
            self.part[t, self.core, lo : lo + R // 2] = total[lo : lo + R // 2] + self.relay_rx[i]
            self.x_copy(i).start()
        else:
            self.part[t, self.core] = total

    def x_sum(self, t):
        total = self.part[t, self.core]
        for i in (t - 6, t - 4):
            self.x_copy(i).wait_recv()
            total = total + self.x_rx[i]
        return total

    def x_done(self):
        self.part[6, self.core] = self.x_sum(6)
        self.yl_copy().start()
        self.part[7, self.core] = self.x_sum(7)

    def yl_done(self):
        self.yl_copy().wait_recv()
        total = self.part[7, self.core] + self.yl_rx[...]
        self.z_tx[...] = total.reshape(NZ, ZR, 128)
        for i in (4, 3, 5, 2, 6, 1, 7):
            self.z_copy(i).start()

    def z_copy(self, i):
        zz, peer = self.z_peer(i)
        return self.to(self.z_tx.at[zz], self.z_rx.at[i], 3, i, peer, self.own)

    def y_copy(self, i):
        return remote(self.y_tx, self.y_rx.at[i], self.sems_y.at[0, i], self.sems_y.at[1, i], self.y_peer(i), self.own)

    def z_done(self):
        acc = self.z_tx[self.z]
        for i in range(1, NZ):
            self.z_copy(i).wait_recv()
            acc = acc + self.z_rx[i]
        self.y_tx[...] = acc
        for i in (2, 1, 3):
            self.y_copy(i).start()

    def gather_copy(self, i):
        block = self.fin.at[self.core, self.z]
        return self.to(block, block, 4, i, self.z_peer(i)[1], self.own)

    def from_z(self, core, i):
        return self.fin.at[core, lax.rem(self.z + NZ - i, NZ)]

    def arrival(self, i):
        block = self.from_z(self.core, i)
        return self.to(block, block, 4, i, self.z_peer(i)[1], self.own)

    def twin_copy(self, i):
        block = self.from_z(self.core, i)
        return self.to(block, block, 5, i, self.sib, self.own)

    def twin_arrival(self, i):
        block = self.from_z(1 - self.core, i)
        return self.to(block, block, 5, i, self.sib, self.own)

    def y_done(self):
        acc = self.y_tx[...]
        for i in range(1, NY):
            self.y_copy(i).wait_recv()
            acc = acc + self.y_rx[i]
        self.fin[self.core, self.z] = acc
        for i in (4, 3, 5, 2, 6, 1, 7):
            self.gather_copy(i).start()
        self.twin_copy(0).start()

    def gather_done(self):
        for i in (1, 7, 2, 6, 3, 5, 4):
            self.arrival(i).wait_recv()
            self.twin_copy(i).start()

    def twin_done(self):
        for i in range(NZ):
            self.twin_arrival(i).wait_recv()

    def drain(self):
        for t in range(LAYERS):
            self.core_copy(t).wait_send()
        for i in range(4):
            self.relay(i).wait_send()
            self.x_copy(i).wait_send()
        self.yl_copy().wait_send()
        for i in range(1, NZ):
            self.z_copy(i).wait_send()
            self.gather_copy(i).wait_send()
        for i in range(1, NY):
            self.y_copy(i).wait_send()
        for i in range(NZ):
            self.twin_copy(i).wait_send()


def split3(x):
    a = x.astype(bf16)
    r = x - a.astype(f32)
    b = r.astype(bf16)
    r = r - b.astype(f32)
    return a, b, r.astype(bf16)


def outer(p, r):
    p1, p2, p3 = split3(p)
    r1, r2, r3 = split3(r)
    lhs = jnp.concatenate([p1, p1, p2, p2, p1, p3], 0)
    rhs = jnp.concatenate([r1, r2, r1, r2, r3, r1], 0)
    return lax.dot_general(lhs, rhs, (((0,), (0,)), ((), ())), preferred_element_type=f32)


class Sweep:
    def __init__(self, ref, n):
        self.ref, self.n, self.ahead = ref, n, None

    def load(self, k):
        rows = self.ref[8 * k : 8 * k + 8, :]
        return [rows[:, 128 * c : 128 * c + 128] for c in range(self.n // 128)]

    def panel(self, k):
        lo, n = 8 * k, self.n
        kc, kl = lo // 128, lo % 128
        sub = lax.broadcasted_iota(jnp.int32, (8, 128), 0)
        lane = lax.broadcasted_iota(jnp.int32, (8, 128), 1)
        chunks = self.load(k) if self.ahead is None else self.ahead
        rows = jnp.concatenate(chunks, 1) if n > 128 else chunks[0]

        def column(x, j):
            return jnp.broadcast_to(x[:, j : j + 1], (8, 128))

        def row(x, j):
            return jnp.broadcast_to(x[j : j + 1, :], (8, 128))

        cols = [column(chunks[kc], kl + j) for j in range(8)]
        more = lo + 8 < n
        if more:
            raw = self.load(k + 1)
            weights = [column(raw[kc], kl + m) for m in range(8)]
        for p in range(8):
            rec = 1.0 / row(cols[p], p)
            factor = cols[p]
            here = sub == p
            chunks = list(chunks)
            chunks[kc] = jnp.where(lane == kl + p, jnp.where(here, 1.0, 0.0), chunks[kc])

            def step(x):
                scaled = row(x, p) * rec
                return jnp.where(here, scaled, x - factor * scaled)

            cols = [step(cols[j]) if j > p else cols[j] for j in range(8)]
            chunks = [step(x) for x in chunks]
        inside = (lane >= kl) & (lane < kl + 8)
        chunks[kc] = jnp.where(inside, -chunks[kc], chunks[kc])
        swept = jnp.concatenate(chunks, 1) if n > 128 else chunks[0]
        if more:
            self.ahead = []
            for c in range(n // 128):
                old = jnp.where(inside, 0.0, raw[c]) if c == kc else raw[c]
                t = [weights[m] * row(chunks[c], m) for m in range(8)]
                self.ahead.append(old - (((t[0] + t[1]) + (t[2] + t[3])) + ((t[4] + t[5]) + (t[6] + t[7]))))
        change = outer(rows, swept)
        lanes = lax.broadcasted_iota(jnp.int32, (1, n), 1)
        own_cols = (lanes >= lo) & (lanes < lo + 8)
        self.ref[...] = jnp.where(own_cols, 0.0, self.ref[...]) - change
        self.ref[lo : lo + 8, :] = swept


def eye(n):
    i = lax.broadcasted_iota(jnp.int32, (n, n), 0)
    j = lax.broadcasted_iota(jnp.int32, (n, n), 1)
    return jnp.where(i == j, 1.0, 0.0).astype(f32)


def main_kernel(scale, wide_hbm, narrow_hbm, out_ref, wbuf, nbuf, in_sem, a_ref, n_ref, cols_ref, x_sem, *refs):
    first, second = Stream(refs[:12]), Stream(refs[12:])
    dp, own, z, yh, core = place()

    def loads(t):
        l = first.layer_of(t)
        return (
            pltpu.make_async_copy(wide_hbm.at[l], wbuf.at[t], in_sem.at[0, t]),
            pltpu.make_async_copy(narrow_hbm.at[l], nbuf.at[t], in_sem.at[1, t]),
        )

    for part in range(2):
        for t in range(LAYERS):
            loads(t)[part].start()

    def own_peer(i):
        return lax.rem(own + i, NO)

    barrier = pltpu.get_barrier_semaphore()

    def greet(dp, own):
        pl.semaphore_signal(barrier, inc=1, device_id=(dp, own), device_id_type=MESH)

    greet(first.sib, own)
    for i in range(1, NO):
        greet(dp, own_peer(i))
    for i in range(1, NZ):
        greet(first.z_peer(i)[1], own)
    for i in range(1, NY):
        greet(first.y_peer(i), own)

    def stats_first(t):
        loads(t)[0].wait()
        wide = wbuf[t]
        right = wide[:, 128:]
        top = gram(wide[:, :128], wide)
        first.part[t, 0, 0:128, :] = top[:, :128]
        first.part[t, 0, 128:192, :] = top[0:64, 128:]
        first.part[t, 1, 0:64, :] = top[64:128, 128:]
        first.part[t, 1, 64:192, :] = gram(right, right)

    def stats_second(t):
        loads(t)[1].wait()
        narrow = nbuf[t]
        mixed = gram(narrow, wbuf[t])
        second.part[t, 0, 0:128, :] = gram(narrow, narrow)
        second.part[t, 0, 128:192, :] = mixed[0:64, :128]
        second.part[t, 1, 0:64, :] = mixed[64:128, :128]
        second.part[t, 1, 64:192, :] = mixed[:, 128:]

    stats_first(0)
    pl.semaphore_wait(barrier, 1 + (NO - 1) + (NZ - 1) + (NY - 1))
    first.core_copy(0).start()
    for t in range(1, LAYERS):
        stats_first(t)
        first.core_copy(t).start()
        first.pass_on(t - 1)
    stats_second(0)
    second.core_copy(0).start()
    first.pass_on(LAYERS - 1)
    for t in range(1, LAYERS):
        stats_second(t)
        second.core_copy(t).start()
        second.pass_on(t - 1)
    second.pass_on(LAYERS - 1)
    first.x_done()
    first.yl_done()
    second.x_done()
    first.z_done()
    second.yl_done()
    first.y_done()
    second.z_done()
    first.gather_done()
    first.twin_done()
    second.y_done()

    damp = DAMP * eye(128)
    wide = first.fin[...].reshape(384, 128) * scale
    cross = wide[128:256]
    a_ref[0:128, 0:128] = wide[0:128] + damp
    a_ref[0:128, 128:256] = cross
    a_ref[128:256, 0:128] = cross.T
    a_ref[128:256, 128:256] = wide[256:384] + damp
    a_sweep, n_sweep = Sweep(a_ref, WIDE), Sweep(n_ref, NARROW)
    late = (WIDE - NARROW) // 8
    for k in range(WIDE // 8):
        a_sweep.panel(k)
        if k == late - 2:
            second.gather_done()
        if k == late - 1:
            second.twin_done()
            n_ref[...] = second.fin[...].reshape(384, 128)[0:128] * scale + damp
        if k >= late:
            n_sweep.panel(k - late)
    x = -a_ref[pl.ds(pl.multiple_of(dp // 2 * 8, 8), 8), :]
    last = (((1,), (1,)), ((), ()))
    mixed = second.fin[...].reshape(384, 128)[128:384] * scale
    inner = 0.0
    for b in range(2):
        half = mixed[128 * b : 128 * b + 128]
        inner = inner + lax.dot_general(x[:, 128 * b : 128 * b + 128], half, last, precision=HI, preferred_element_type=f32)
    u = -jnp.dot(inner, n_ref[...], precision=HI, preferred_element_type=f32)
    both = jnp.concatenate([x, u], 1)
    cols_ref[...] = jnp.where(core == 0, both[0:4], both[4:8])

    def copy(i):
        return remote(cols_ref, out_ref.at[own], x_sem.at[0, i], x_sem.at[1, i], dp, own_peer(i))

    def arrival(i):
        return remote(cols_ref, out_ref.at[own_peer(NO - i)], x_sem.at[0, i], x_sem.at[1, i], dp, own_peer(i))

    for i in range(1, NO):
        copy(i).start()
    out_ref[own] = cols_ref[...]
    first.drain()
    second.drain()
    for i in range(1, NO):
        arrival(i).wait_recv()
    for i in range(1, NO):
        copy(i).wait_send()


def columns(wide_rows, narrow_rows, total):
    vmem, dma = pltpu.VMEM, pltpu.SemaphoreType.DMA
    return pl.pallas_call(
        functools.partial(main_kernel, 1.0 / total),
        out_shape=jax.ShapeDtypeStruct((NO, 4, WIDE + NARROW), f32),
        in_specs=[pl.BlockSpec(memory_space=pltpu.HBM)] * 2,
        out_specs=pl.BlockSpec(memory_space=pltpu.VMEM),
        scratch_shapes=[
            vmem((LAYERS, ROWS, WIDE), bf16), vmem((LAYERS, ROWS, NARROW), bf16), dma((2, LAYERS)),
            vmem((WIDE, WIDE), f32), vmem((NARROW, NARROW), f32), vmem((4, WIDE + NARROW), f32), dma((2, NO)),
            *Stream.scratch(), *Stream.scratch(),
        ],
        compiler_params=pltpu.CompilerParams(
            collective_id=0, has_side_effects=True, vmem_limit_bytes=60 << 20
        ),
    )(wide_rows, narrow_rows)


def select_kernel(owners, cols_ref, kept_ref, update_ref):
    dp, own, _, _, _ = place()
    i0 = lax.broadcasted_iota(jnp.int32, (4, WIDE), 0)
    i1 = lax.broadcasted_iota(jnp.int32, (4, WIDE), 1)
    empty = jnp.where(i1 == dp * 4 + i0, 1.0 / DAMP, 0.0).astype(f32)
    kept = [empty, empty]
    shift = lax.rem(128 - 16 * own, 128)
    for l in range(LAYERS):
        slot = owners[l] * 2
        for j in range(l):
            slot = slot + jnp.where(owners[j] == owners[l], 1, 0)
        got = cols_ref[l]
        kept = [jnp.where(slot == own * 2 + c, got[:, :WIDE], kept[c]) for c in range(2)]
        part = jnp.concatenate([got[:, WIDE:], got[:, WIDE:]], 0)
        update_ref[l] = pltpu.roll(part, shift, 1)[0:4, 0:16]
    kept_ref[0] = kept[0]
    kept_ref[1] = kept[1]


def select(owner_map, cols):
    vmem = pl.BlockSpec(memory_space=pltpu.VMEM)
    return pl.pallas_call(
        select_kernel,
        out_shape=(
            jax.ShapeDtypeStruct((2, 4, WIDE), f32),
            jax.ShapeDtypeStruct((LAYERS, 4, 16), f32),
        ),
        in_specs=[pl.BlockSpec(memory_space=pltpu.SMEM), vmem],
        out_specs=(vmem, vmem),
    )(owner_map, cols)


def on_device(wide_rows, narrow_rows, owner_map):
    cols = columns(wide_rows, narrow_rows, ROWS * 512)
    kept, update = select(owner_map, cols)
    return kept.transpose(0, 2, 1), update.transpose(0, 2, 1)


def solution(mesh):
    in_specs = (P(None, ("dp", "own"), None), P(None, ("dp", "own"), None), P())
    out_specs = (P("own", None, "dp"), P(None, "own", "dp"))
    return jax.shard_map(
        on_device, mesh=mesh, in_specs=in_specs, out_specs=out_specs, check_vma=False
    )
```

time: 80.1 us -> 70.3 us (0.88)
  Pallas kernels: 79 us -> 69.5 us
    pallas_call x1, Pallas kernels: 77.5 us -> 68 us  [columns(): pl.pallas_call(functools.partial(main_kernel, 1.0 / total), out_shape=jax...]
where the time goes in v3:
time: 70.3 us; the launch traced here: 70.2 us
  Pallas kernels  69.5 us (99%)
    pallas_call x1, Pallas kernels, columns(): pl.pallas_call(functools.partial(main_kernel, 1.0 / total), out_shape=jax...  68 us
    pallas_call x1, Pallas kernels, select(): pl.pallas_call(select_kernel, out_shape=(jax.ShapeDtypeStruct((2, 4, WIDE...  1.5 us

profile of v3, /device:TPU:1, one launch (start us, length us, event | category | flops | bytes accessed | tf_op | source)
XLA Modules:
  0.0 70.2 jit_solution(6129546699132886431)
XLA Ops:
  0.6 68.0 %shard_map.50.cols_ref = f32[8,4,384]{2,1,0:T(4,128)} custom-call(bf16[8,768,256]{2,1,0:T(8,128)(2,1)} %wide_hbm.1, bf16[8,768,128]{2,1,0:T(8,128)(2,1)} %narrow_hbm.1), custom_call_target="tpu_custom_call" | custom-call | tf_op jit(solution)/shard_map/pallas_call | solution.py:402
  68.7 1.5 %shard_map.51 = (f32[2,4,256]{2,1,0:T(4,128)}, f32[8,4,16]{2,1,0:T(4,128)}) custom-call(s32[8]{0:T(128)} %owners.1, f32[8,4,384]{2,1,0:T(4,128)} %shard_map.50.cols_ref), custom_call_target="tpu_custom_call" | custom-call | tf_op jit(solution)/shard_map/pallas_call | solution.py:439

commit v4 on v3

--- a/solution.py
+++ b/solution.py
@@ -33,6 +33,7 @@
 
 R = 192
 ZR = R // NZ
+LAG = 3
 DX = (2, 2, 1, 1, 3, 3, 0, 0)
 
 
@@ -331,22 +332,24 @@
     for t in range(1, LAYERS):
         stats_first(t)
         first.core_copy(t).start()
-        first.pass_on(t - 1)
-    stats_second(0)
-    second.core_copy(0).start()
-    first.pass_on(LAYERS - 1)
-    for t in range(1, LAYERS):
+        if t >= LAG:
+            first.pass_on(t - LAG)
+    for t in range(LAYERS):
         stats_second(t)
         second.core_copy(t).start()
-        second.pass_on(t - 1)
-    second.pass_on(LAYERS - 1)
+        if t < LAG:
+            first.pass_on(LAYERS - LAG + t)
+        else:
+            second.pass_on(t - LAG)
+    for t in range(LAYERS - LAG, LAYERS):
+        second.pass_on(t)
     first.x_done()
     first.yl_done()
     second.x_done()
+    second.yl_done()
     first.z_done()
-    second.yl_done()
+    second.z_done()
     first.y_done()
-    second.z_done()
     first.gather_done()
     first.twin_done()
     second.y_done()

time: 70.3 us -> 68.7 us (0.977)
  Pallas kernels: 69.5 us -> 67.9 us
    pallas_call x1, Pallas kernels: 68 us -> 66.4 us  [columns(): pl.pallas_call(functools.partial(main_kernel, 1.0 / total), out_shape=jax...]
where the time goes in v4:
time: 68.7 us; the launch traced here: 68.5 us
  Pallas kernels  67.9 us (99%)
    pallas_call x1, Pallas kernels, columns(): pl.pallas_call(functools.partial(main_kernel, 1.0 / total), out_shape=jax...  66.4 us
    pallas_call x1, Pallas kernels, select(): pl.pallas_call(select_kernel, out_shape=(jax.ShapeDtypeStruct((2, 4, WIDE...  1.5 us

profile of v4, /device:TPU:1, one launch (start us, length us, event | category | flops | bytes accessed | tf_op | source)
XLA Modules:
  0.0 68.5 jit_solution(16431185526922576551)
XLA Ops:
  0.6 66.4 %shard_map.50.cols_ref = f32[8,4,384]{2,1,0:T(4,128)} custom-call(bf16[8,768,256]{2,1,0:T(8,128)(2,1)} %wide_hbm.1, bf16[8,768,128]{2,1,0:T(8,128)(2,1)} %narrow_hbm.1), custom_call_target="tpu_custom_call" | custom-call | tf_op jit(solution)/shard_map/pallas_call | solution.py:405
  67.0 1.5 %shard_map.51 = (f32[2,4,256]{2,1,0:T(4,128)}, f32[8,4,16]{2,1,0:T(4,128)}) custom-call(s32[8]{0:T(128)} %owners.1, f32[8,4,384]{2,1,0:T(4,128)} %shard_map.50.cols_ref), custom_call_target="tpu_custom_call" | custom-call | tf_op jit(solution)/shard_map/pallas_call | solution.py:442

commit v5 on v4

--- a/solution.py
+++ b/solution.py
@@ -33,7 +33,7 @@
 
 R = 192
 ZR = R // NZ
-LAG = 3
+LAG = 4
 DX = (2, 2, 1, 1, 3, 3, 0, 0)
 
 
@@ -389,7 +389,7 @@
     def arrival(i):
         return remote(cols_ref, out_ref.at[own_peer(NO - i)], x_sem.at[0, i], x_sem.at[1, i], dp, own_peer(i))
 
-    for i in range(1, NO):
+    for i in (6, 2, 5, 7, 1, 3, 4):
         copy(i).start()
     out_ref[own] = cols_ref[...]
     first.drain()

time: 68.7 us -> 68.9 us (level)
  no operation moved by 1% of the time
where the time goes in v5:
time: 68.9 us; the launch traced here: 68.8 us
  Pallas kernels  68.1 us (99%)
    pallas_call x1, Pallas kernels, columns(): pl.pallas_call(functools.partial(main_kernel, 1.0 / total), out_shape=jax...  66.6 us
    pallas_call x1, Pallas kernels, select(): pl.pallas_call(select_kernel, out_shape=(jax.ShapeDtypeStruct((2, 4, WIDE...  1.5 us

profile of v5, /device:TPU:1, one launch (start us, length us, event | category | flops | bytes accessed | tf_op | source)
XLA Modules:
  0.0 68.8 jit_solution(12801778848863078928)
XLA Ops:
  0.6 66.6 %shard_map.50.cols_ref = f32[8,4,384]{2,1,0:T(4,128)} custom-call(bf16[8,768,256]{2,1,0:T(8,128)(2,1)} %wide_hbm.1, bf16[8,768,128]{2,1,0:T(8,128)(2,1)} %narrow_hbm.1), custom_call_target="tpu_custom_call" | custom-call | tf_op jit(solution)/shard_map/pallas_call | solution.py:405
  67.3 1.5 %shard_map.51 = (f32[2,4,256]{2,1,0:T(4,128)}, f32[8,4,16]{2,1,0:T(4,128)}) custom-call(s32[8]{0:T(128)} %owners.1, f32[8,4,384]{2,1,0:T(4,128)} %shard_map.50.cols_ref), custom_call_target="tpu_custom_call" | custom-call | tf_op jit(solution)/shard_map/pallas_call | solution.py:442
